TPU v7x, 128 devices: a whole 4x4x4 slice. The times are simulated.
128 devices in a mesh: tm: 32 (over x, z, core), panel: 4 (over y).
Axes of the slice: x: 4, y: 4, z: 4, core: 2. Of those that a mesh axis runs over, the one named last changes fastest.
Arguments:
- design: bfloat16 [8192, 7680], P('tm', 'panel'), may hold values from -6 to 6
- partials: bfloat16 [8192, 64], P('tm'), may hold values from -0.119628906 to 0.119628906
- observed: bfloat16 [8192], P('tm'), may hold values from -6 to 6
- arc_of_row: int32 [8192, 1], replicated, may hold values from 0 to 31, as said below
- autoreg: float32 [32], replicated, may hold values from -0.55 to 0.5
- movavg: float32 [32], replicated, may hold values from 0.3 to 0.9
Outputs:
- normal: float32 [7680, 7680], P('tm', 'panel')
- right_hand: float32 [7680], P('panel')
Inputs may be any that keep to these rules, and one draw needn't show every extreme that they name: arc_of_row never falls along the epochs and names every arc; arcs 2b and 2b + 1 together have 2 * 256 epochs, one of them 384 // 3 to 160 epochs and the other 352 to 384; one arc has exactly 384 epochs and its partner exactly 128, so that at most 12 rows of one device belong to one arc, and every device holds exactly 12 rows of the longest arc; arc a is held by index a of tm.
All inputs are finite; a program needn't handle non-finite values.
Results may differ from a plain program's by a relative error of at most 0.02.
Values may be sent and summed in bfloat16 or wider, within the bound.
A program may use at most 192 MiB of HBM per device.

v0:
```python
import jax
import jax.numpy as jnp
from jax import lax
from jax.sharding import Mesh, PartitionSpec as P

TM = ("tmc", "core")


def whiten_matrix(order_row, order_col, usable_row, usable_col, ar_value, ma_value):
    spacing = order_row[:, None] - order_col[None, :]
    lag_steps = jnp.maximum(spacing - 1, 0)
    parity = (lag_steps % 2).astype(jnp.float32)
    flip_sign = 1.0 - 2.0 * parity
    decayed = (
        -(ar_value + ma_value)
        * flip_sign
        * jnp.exp(lag_steps.astype(jnp.float32) * jnp.log(ma_value))
    )
    entry = jnp.where(spacing == 0, jnp.float32(1.0), decayed)
    allowed = usable_row[:, None] & usable_col[None, :] & (spacing >= 0)
    return jnp.where(allowed, entry, jnp.float32(0.0)).astype(jnp.bfloat16)


def eliminate(whitener, rows_design, rows_params, rows_obs, scale):
    white_design = jnp.dot(whitener, rows_design, preferred_element_type=jnp.float32)
    white_params = jnp.dot(whitener, rows_params, preferred_element_type=jnp.float32)
    white_obs = jnp.dot(whitener, rows_obs, preferred_element_type=jnp.float32)
    param_count = rows_params.shape[1]
    param_gram = jnp.dot(white_params.T, white_params, precision=lax.Precision.HIGHEST) + jnp.eye(
        param_count, dtype=jnp.float32
    )
    factor = jnp.linalg.cholesky(param_gram)
    basis = lax.linalg.triangular_solve(factor, white_params.T, left_side=True, lower=True)
    arc_terms = jnp.dot(basis, white_design, precision=lax.Precision.HIGHEST)
    arc_rhs = jnp.dot(basis, white_obs, precision=lax.Precision.HIGHEST)
    right_part = (
        jnp.dot(white_design.T, white_obs, precision=lax.Precision.HIGHEST)
        - jnp.dot(arc_terms.T, arc_rhs, precision=lax.Precision.HIGHEST)
    ) * scale
    return (white_design.astype(jnp.bfloat16), basis, right_part)


def body(design, partials, observed, arc_of_row, autoreg, movavg):
    chip_count = lax.axis_size("tmc")
    core_count = lax.axis_size("core")
    core_index = lax.axis_index("core")
    tile_count = chip_count * core_count
    device_index = lax.axis_index("tmc") * core_count + core_index
    rows_dev = design.shape[0]
    panel_width = design.shape[1]
    param_count = partials.shape[1]
    capacity = 3 * rows_dev // 2 // tile_count
    slot_count = tile_count * capacity
    scale = 1.0 / (rows_dev * tile_count)
    arc_ids = arc_of_row[:, 0]
    epoch_table = arc_ids.reshape(rows_dev, tile_count)
    local_arcs = lax.dynamic_slice_in_dim(epoch_table, device_index, 1, 1)[:, 0]
    row_id = jnp.arange(rows_dev, dtype=jnp.int32)
    same_arc = local_arcs[:, None] == local_arcs[None, :]
    within = jnp.sum((same_arc & (row_id[None, :] < row_id[:, None])).astype(jnp.int32), axis=1)
    target_slot = local_arcs * capacity + within
    chooser = (target_slot[None, :] == jnp.arange(slot_count, dtype=jnp.int32)[:, None]).astype(
        jnp.bfloat16
    )

    def pick_rows(values):
        picked = jnp.dot(chooser, values, preferred_element_type=jnp.float32)
        return picked.astype(values.dtype)

    send_design = pick_rows(design).reshape(tile_count, capacity, panel_width)
    with_obs = jnp.concatenate([partials, observed[:, None]], axis=1)
    send_params = pick_rows(with_obs).reshape(tile_count, capacity, param_count + 1)
    got_params = lax.all_to_all(send_params, TM, split_axis=0, concat_axis=0, tiled=True)
    send_design, got_params = lax.optimization_barrier((send_design, got_params))
    got_design = lax.all_to_all(send_design, TM, split_axis=0, concat_axis=0, tiled=True)
    got_design = got_design.reshape(slot_count, panel_width)
    got_params = got_params.reshape(slot_count, param_count + 1)
    got_obs = got_params[:, param_count]
    got_params = got_params[:, :param_count]
    per_source = jnp.sum((epoch_table == device_index).astype(jnp.int32), axis=0)
    arc_start = jnp.sum((arc_ids < device_index).astype(jnp.int32))
    first_pos = jnp.mod(jnp.arange(tile_count, dtype=jnp.int32) - arc_start, tile_count)
    offset_in = jnp.arange(capacity, dtype=jnp.int32)
    order_pos = (first_pos[:, None] + offset_in[None, :] * tile_count).reshape(slot_count)
    usable = (offset_in[None, :] < per_source[:, None]).reshape(slot_count)
    position = jnp.arange(slot_count, dtype=jnp.int32)
    arc_length = jnp.sum(per_source)
    whitener = whiten_matrix(
        position,
        order_pos,
        position < arc_length,
        usable,
        autoreg[device_index],
        movavg[device_index],
    )
    design_bf, basis, right_part = eliminate(whitener, got_design, got_params, got_obs, scale)
    swap = [(0, 1), (1, 0)]
    short_most = 5 * rows_dev // 8
    keep = (slot_count + short_most) // 2
    moved = lax.ppermute(design_bf[keep:], "core", swap)
    packed = design_bf[:keep].at[short_most : short_most + moved.shape[0]].add(moved)
    got_basis = lax.ppermute(basis, "core", swap)
    packed, right_part, got_basis = lax.optimization_barrier((packed, right_part, got_basis))
    gathered = lax.all_gather(packed, "panel", axis=1, tiled=True)
    right_hand = lax.psum(right_part + lax.ppermute(right_part, "core", swap), "tmc")
    gathered, right_hand = lax.optimization_barrier((gathered, right_hand))
    half = panel_width // core_count
    got_rows = lax.ppermute(gathered, "core", swap)
    moved_count = slot_count - keep

    def spread(own_basis):
        lead = own_basis[:, :keep]
        tail = jnp.pad(own_basis[:, keep:], ((0, 0), (short_most, keep - short_most - moved_count)))
        return (lead, tail)

    own_lead, own_tail = spread(basis)
    far_lead, far_tail = spread(got_basis)
    stacked_basis = jnp.concatenate(
        [
            jnp.concatenate([own_lead, own_tail], axis=1),
            jnp.concatenate([far_tail, far_lead], axis=1),
        ],
        axis=0,
    ).astype(jnp.bfloat16)
    design_side = jnp.concatenate([gathered, got_rows], axis=0)
    own_share = jnp.dot(stacked_basis[:, :keep], gathered, preferred_element_type=jnp.float32)
    far_share = jnp.dot(stacked_basis[:, keep:], got_rows, preferred_element_type=jnp.float32)
    terms = (own_share + far_share).astype(jnp.bfloat16)
    row_side = jnp.concatenate([design_side, -terms], axis=0)
    col_side = lax.dynamic_slice_in_dim(
        jnp.concatenate([design_side, terms], axis=0),
        lax.axis_index("panel") * panel_width + core_index * half,
        half,
        1,
    )
    product = lax.dot_general(
        row_side, col_side, (((0,), (0,)), ((), ())), preferred_element_type=jnp.float32
    )
    pair = lax.psum_scatter(
        (product * scale).astype(jnp.bfloat16), "tmc", scatter_dimension=0, tiled=True
    )
    block_rows = pair.shape[0] // core_count
    by_core = pair.reshape(core_count, block_rows, half)
    mine = jnp.where(core_index == 0, by_core[0], by_core[1])
    given = jnp.where(core_index == 0, by_core[1], by_core[0])
    got = lax.ppermute(given, "core", swap)
    first = jnp.where(core_index == 0, mine, got)
    second = jnp.where(core_index == 0, got, mine)
    normal = jnp.concatenate([first, second], axis=1).astype(jnp.float32)
    return (normal, right_hand)


def solution(mesh):
    chips = mesh.devices.shape[0] // 2
    split = Mesh(mesh.devices.reshape(chips, 2, mesh.devices.shape[1]), ("tmc", "core", "panel"))
    in_specs = (P(TM, "panel"), P(TM, None), P(TM), P(), P(), P())
    out_specs = (P(TM, "panel"), P("panel"))
    return jax.shard_map(body, mesh=split, in_specs=in_specs, out_specs=out_specs, check_vma=False)
```

profile of v0, /device:TPU:1, one launch (start us, length us, event | category | flops | bytes accessed | tf_op | source)
XLA Modules:
  0.0 268.0 jit_solution(4440556200000650307)
XLA Ops:
  7.2 0.7 broadcast_in_dim.12
  7.9 0.5 broadcast.170
  8.5 2.3 fusion.53
  10.7 0.1 reshape_squeeze.3
  10.8 0.2 dynamic-slice_reduce_fusion
  11.0 0.2 convert_reduce_fusion
  11.2 1.0 convolution_convert_fusion.1
  12.2 0.1 copy.13
  12.3 0.8 reshape.152
  13.1 9.4 %all-to-all-start = ((bf16[32,2,390]{2,1,0:T(2,128)(2,1)}), bf16[32,2,390]{2,1,0:T(2,128)(2,1)S(1)}, u32[]{:S(2)}, u32[]{:S(2)}) async-start(bf16[32,2,390]{2,1,0:T(2,128)(2,1)} %reshape.152), calls=%async_computation | async-start | bytes 131072 | tf_op jit(solution)/shard_map/all_to_all | solution.py:73
  22.6 0.1 convert_reduce_fusion.1
  22.6 0.7 and_select_fusion
  23.3 0.1 iota_compare_fusion.11
  23.4 0.6 convolution_convert_fusion
  24.0 0.1 broadcast_add_fusion
  24.1 0.7 iota_compare_fusion.12
  24.7 0.6 dynamic_slice.13
  26.0 0.7 dynamic_slice.12
  28.1 0.1 add.105
  28.2 0.1 lt.73
  28.3 1.5 reshape.124
  29.7 0.2 all-to-all-done
  29.9 0.2 reshape.153
  30.1 7.2 %all-to-all-start.1 = ((bf16[32,12,1920]{2,1,0:T(8,128)(2,1)}), bf16[32,12,1920]{2,1,0:T(8,128)(2,1)S(1)}, u32[]{:S(2)}, u32[]{:S(2)}) async-start(bf16[32,12,1920]{2,1,0:T(8,128)(2,1)} %reshape.124), calls=%async_computation.1 | async-start | bytes 3932160 | tf_op jit(solution)/shard_map/all_to_all | solution.py:75
  37.4 0.7 fusion.34
  38.1 0.2 fusion.87
  38.3 0.2 slice_reduce_fusion
  38.5 0.1 copy.14
  38.6 5.8 %cholesky.17 = f32[64,64]{1,0:T(8,128)S(1)} custom-call(f32[64,64]{1,0:T(8,128)S(1)} %fusion.58), custom_call_target="Cholesky" | custom-call | tf_op jit(solution)/shard_map/jit(cholesky)/cholesky | solution.py:32
  44.5 0.6 compare_reduce_fusion
  45.2 0.7 fusion.52
  45.8 4.9 %custom-call.6 = f32[1,64,64]{1,2,0:T(8,128)S(1)} custom-call(f32[1,64,64]{2,1,0:T(8,128)S(1)} %fusion.52), custom_call_target="InvertDiagBlocksLowerTriangular" | custom-call | tf_op jit(solution)/shard_map/triangular_solve | solution.py:33
  50.7 0.3 fusion.84
  51.0 0.3 collective-permute-start.1
  51.3 0.6 convolution_bitcast_fusion
  52.0 0.2 convolution_bitcast_fusion.1
  52.2 12.0 %all-to-all-done.1 = bf16[32,12,1920]{2,1,0:T(8,128)(2,1)S(1)} async-done(((bf16[32,12,1920]{2,1,0:T(8,128)(2,1)}), bf16[32,12,1920]{2,1,0:T(8,128)(2,1)S(1)}, u32[]{:S(2)}, u32[]{:S(2)}) %all-to-all-start.1) | async-done | bytes 1474592 | tf_op jit(solution)/shard_map/all_to_all | solution.py:75
  64.2 1.3 reshape.126
  65.5 2.8 %fusion.85 = (bf16[384,1920]{1,0:T(8,128)(2,1)S(1)}, f32[384,1920]{1,0:T(8,128)S(1)}) fusion(bf16[384,1920]{1,0:T(8,128)(2,1)} %reshape.126, f32[]{:T(128)} %bitcast.1, f32[]{:T(128)} %bitcast, s32[384]{0:T(512)S(1)} %add.105, pred[384]{0:T(512)(128)(4,1)S(1)} %lt.73, pred[384]{0:T(512)(128)(4,1)S(1)} %iota_compare_fusion.12), kind=kOutput, calls=%fused_computation.126 | convolution fusion | flops 570359808 | bytes 5900552 | tf_op jit(solution)/shard_map/dot_general | solution.py:25
  68.3 0.1 slice.87
  68.4 1.8 fusion.88
  70.2 1.1 collective-permute-start
  71.3 0.4 convolution_reduce_fusion
  71.7 1.7 fusion.9
  73.4 0.1 fusion.27
  73.6 0.9 copy-done.2
  74.6 0.1 collective-permute-start.2
  74.7 1.2 collective-permute-done.2
  75.8 30.8 %psum.7 = f32[1920]{0:T(1024)} all-reduce(f32[1920]{0:T(1024)S(1)} %add.114), channel_id=1, replica_groups=mesh['tmc'=16,'core'=2,'panel'=4] {'tmc'}, use_global_device_ids=true, to_apply=%region_6.7 | all-reduce | flops 1920 | bytes 15360 | tf_op jit(solution)/shard_map/psum | solution.py:105
  106.6 13.1 %all-gather.2.cloned.1.call-done = bf16[272,7680]{1,0:T(8,128)(2,1)} async-done(((bf16[272,1920]{1,0:T(8,128)(2,1)}), bf16[272,7680]{1,0:T(8,128)(2,1)}) %all-gather.2.cloned.1.call-update) | async-done | bytes 4177936 | tf_op jit(solution)/shard_map/all_gather | solution.py:104
  119.7 0.7 collective-permute-start.3
  120.5 0.1 slice.93
  120.5 0.1 slice.94
  120.6 0.1 fusion.43
  120.7 3.4 %fusion.46 = f32[128,7680]{1,0:T(8,128)S(1)} fusion(bf16[272,7680]{1,0:T(8,128)(2,1)} %all-gather.2.cloned.1.call-done, bf16[128,544]{1,0:T(8,128)(2,1)S(1)} %fusion.43), kind=kOutput, calls=%fused_computation.70 | convolution fusion | flops 534773760 | bytes 8208384 | tf_op jit(solution)/shard_map/dot_general | solution.py:126
  124.1 3.5 %collective-permute-done.3 = bf16[272,7680]{1,0:T(8,128)(2,1)} collective-permute-done((bf16[272,7680]{1,0:T(8,128)(2,1)}, bf16[272,7680]{1,0:T(8,128)(2,1)}, u32[]{:S(2)}, u32[]{:S(2)}) %collective-permute-start.3) | collective-permute-done | bytes 4177952 | tf_op jit(solution)/shard_map/ppermute | solution.py:108
  127.6 3.4 %fusion.86 = (bf16[128,7680]{1,0:T(8,128)(2,1)S(1)}, bf16[128,7680]{1,0:T(8,128)(2,1)S(1)}) fusion(f32[128,7680]{1,0:T(8,128)S(1)} %fusion.46, bf16[272,7680]{1,0:T(8,128)(2,1)} %collective-permute-done.3, bf16[128,544]{1,0:T(8,128)(2,1)S(1)} %fusion.43), kind=kOutput, calls=%fused_computation.127 | convolution fusion | flops 537722880 | bytes 12140544 | tf_op jit(solution)/shard_map/dot_general | solution.py:127
  131.0 18.2 %multiply_convert_fusion = bf16[7680,960]{1,0:T(8,128)(2,1)} fusion(bf16[272,7680]{1,0:T(8,128)(2,1)} %collective-permute-done.3, bf16[272,7680]{1,0:T(8,128)(2,1)S(1)} %copy-done.1, bf16[128,7680]{1,0:T(8,128)(2,1)S(1)} %get-tuple-element.38, s32[]{:T(128)S(6)} %select_n.64, bf16[128,7680]{1,0:T(8,128)(2,1)S(1)} %get-tuple-element.39), kind=kOutput, calls=%fused_computation | convolution fusion | flops 9958625280 | bytes 35389444 | tf_op jit(solution)/shard_map/dot_general | solution.py:136
  149.2 105.4 %reduce-scatter.2.cloned.1.call-done = bf16[480,960]{1,0:T(8,128)(2,1)} async-done(((bf16[7680,960]{1,0:T(8,128)(2,1)}), bf16[480,960]{1,0:T(8,128)(2,1)}) %reduce-scatter.2.cloned.1.call-update) | async-done | bytes 921616 | tf_op jit(solution)/shard_map/reduce_scatter | solution.py:139
  254.6 1.2 broadcast_select_fusion.2
  255.8 1.1 collective-permute-start.4
  256.9 1.5 collective-permute-done.4
  258.4 1.3 broadcast_select_fusion.1
  259.7 1.5 maximum_convert_fusion
  (25 shorter events, 0.3 us)
Async XLA Ops:
  7.2 16.3 %copy-start = (bf16[256,1920]{1,0:T(8,128)(2,1)S(1)}, bf16[256,1920]{1,0:T(8,128)(2,1)}, u32[]{:S(2)}) copy-start(bf16[256,1920]{1,0:T(8,128)(2,1)} %param.8) | copy-start | bytes 2949124
  7.2 17.6 %copy-start.3 = (f32[32]{0:T(128)S(1)}, f32[32]{0:T(128)}, u32[]{:S(2)}) copy-start(f32[32]{0:T(128)} %param.13) | copy-start | bytes 388
  7.2 18.8 %copy-start.4 = (f32[32]{0:T(128)S(1)}, f32[32]{0:T(128)}, u32[]{:S(2)}) copy-start(f32[32]{0:T(128)} %param.12) | copy-start | bytes 388
  13.1 16.8 %all-to-all-start = ((bf16[32,2,390]{2,1,0:T(2,128)(2,1)}), bf16[32,2,390]{2,1,0:T(2,128)(2,1)S(1)}, u32[]{:S(2)}, u32[]{:S(2)}) async-start(bf16[32,2,390]{2,1,0:T(2,128)(2,1)} %reshape.152), calls=%async_computation | async-start | bytes 131072 | tf_op jit(solution)/shard_map/all_to_all | solution.py:73
  30.1 34.1 %all-to-all-start.1 = ((bf16[32,12,1920]{2,1,0:T(8,128)(2,1)}), bf16[32,12,1920]{2,1,0:T(8,128)(2,1)S(1)}, u32[]{:S(2)}, u32[]{:S(2)}) async-start(bf16[32,12,1920]{2,1,0:T(8,128)(2,1)} %reshape.124), calls=%async_computation.1 | async-start | bytes 3932160 | tf_op jit(solution)/shard_map/all_to_all | solution.py:75
  37.3 82.4 %all-gather.2.cloned.1.call-start = ((), (), s32[]{:S(2)}) async-start(), calls=%async_computation.3 | async-start | bytes 5222400 | tf_op jit(solution)/shard_map/all_gather | solution.py:104
  51.0 22.5 %collective-permute-start.1 = (bf16[64,384]{1,0:T(8,128)(2,1)S(1)}, bf16[64,384]{1,0:T(8,128)(2,1)S(1)}, u32[]{:S(2)}, u32[]{:S(2)}) collective-permute-start(bf16[64,384]{1,0:T(8,128)(2,1)S(1)} %get-tuple-element.33), channel_id=1, source_target_pairs={{0,4},{4,0},{1,5},{5,1},{2,6},{6,2},{3,7},{7,3},{8,12},{12,8},{9,1... | collective-permute-start | bytes 147464 | tf_op jit(solution)/shard_map/ppermute | solution.py:102
  70.2 3.2 %collective-permute-start = (bf16[112,1920]{1,0:T(8,128)(2,1)S(1)}, bf16[112,1920]{1,0:T(8,128)(2,1)S(1)}, u32[]{:S(2)}, u32[]{:S(2)}) collective-permute-start(bf16[112,1920]{1,0:T(8,128)(2,1)S(1)} %slice.89), channel_id=1, source_target_pairs={{0,4},{4,0},{1,5},{5,1},{2,6},{6,2},{3,7},{7,3},{8,12},{12,8},{9,1... | collective-permute-start | bytes 1290248 | tf_op jit(solution)/shard_map/ppermute | solution.py:100
  73.5 1.0 copy-start.2
  74.5 180.1 %reduce-scatter.2.cloned.1.call-start = ((), (), s32[]{:S(2)}) async-start(), calls=%async_computation.4 | async-start | bytes 16711680 | tf_op jit(solution)/shard_map/reduce_scatter | solution.py:139
  74.6 1.3 collective-permute-start.2
  119.7 7.8 %collective-permute-start.3 = (bf16[272,7680]{1,0:T(8,128)(2,1)}, bf16[272,7680]{1,0:T(8,128)(2,1)}, u32[]{:S(2)}, u32[]{:S(2)}) collective-permute-start(bf16[272,7680]{1,0:T(8,128)(2,1)} %all-gather.2.cloned.1.call-done), channel_id=1, source_target_pairs={{0,4},{4,0},{1,5},{5,1},{2,6},{6,2},{3,7},{7,3},{8,12},{12,8},{9,1... | collective-permute-start | bytes 12533768 | tf_op jit(solution)/shard_map/ppermute | solution.py:108
  124.1 6.9 %copy-start.1 = (bf16[272,7680]{1,0:T(8,128)(2,1)S(1)}, bf16[272,7680]{1,0:T(8,128)(2,1)}, u32[]{:S(2)}) copy-start(bf16[272,7680]{1,0:T(8,128)(2,1)} %all-gather.2.cloned.1.call-done) | copy-start | bytes 12533764
  255.8 2.6 collective-permute-start.4
Sparse Core Ops, SparseCore 0:
  74.6 45.0 all-gather.1
  149.3 105.1 reduce-scatter.1
where the time goes:
time: 269 us; the launch traced here: 268 us
  waiting for transfers between devices  137 us (51%)
  matrix products  35.2 us (13%)
  blocking collectives  30.8 us (11%)
  other arithmetic  20.3 us (8%)
  starting transfers between devices  20 us (7%)
  between operations  16.4 us (6%)
  local copies, waits for them, and re-layouts  8.41 us (3%)
    reduce_scatter x1, waiting for transfers between devices, body(): lax.psum_scatter((product * scale).astype(jnp.bfloat16), 'tmc', scatter_d...  105 us
    psum x1, blocking collectives, body(): lax.psum(right_part + lax.ppermute(right_part, 'core', swap), 'tmc')  30.8 us
    dot_general x1, matrix products, body(): lax.dot_general(row_side, col_side, (((0,), (0,)), ((), ())), preferred_e...  18.2 us
    all_gather x1, waiting for transfers between devices, body(): gathered = lax.all_gather(packed, 'panel', axis=1, tiled=True)  13.1 us
    all_to_all x1, waiting for transfers between devices, body(): lax.all_to_all(send_design, TM, split_axis=0, concat_axis=0, tiled=True)  12 us
    all_to_all x1, starting transfers between devices, body(): lax.all_to_all(send_params, TM, split_axis=0, concat_axis=0, tiled=True)  9.43 us
    all_to_all x1, starting transfers between devices, body(): lax.all_to_all(send_design, TM, split_axis=0, concat_axis=0, tiled=True)  7.18 us
    another operation x3, other arithmetic, eliminate(): factor = jnp.linalg.cholesky(param_gram)  6.52 us
  transfers between devices with their start and end apart: 9, of which 7 were waited for; matrix products, arithmetic and copies ran while one was open for 12% of the time, Pallas kernels for 0%

commit v1 on v0

--- a/solution.py
+++ b/solution.py
@@ -101,7 +101,9 @@
     packed = design_bf[:keep].at[short_most : short_most + moved.shape[0]].add(moved)
     got_basis = lax.ppermute(basis, "core", swap)
     packed, right_part, got_basis = lax.optimization_barrier((packed, right_part, got_basis))
-    gathered = lax.all_gather(packed, "panel", axis=1, tiled=True)
+    gathered = jnp.concatenate(
+        lax.all_to_all(jnp.stack([packed] * lax.axis_size("panel")), "panel", 0, 0), axis=1
+    )
     right_hand = lax.psum(right_part + lax.ppermute(right_part, "core", swap), "tmc")
     gathered, right_hand = lax.optimization_barrier((gathered, right_hand))
     half = panel_width // core_count

time: 269 us -> 279 us (1.037)
  local copies, waits for them, and re-layouts: 8.41 us -> 14.2 us
  starting transfers between devices: 20 us -> 24.8 us
    all_to_all x0 -> x1, waiting for transfers between devices: none -> 16.8 us  [body(): lax.all_to_all(jnp.stack([packed] * lax.axis_size('panel')), 'panel', 0, 0)]
    all_gather x1 -> x0, waiting for transfers between devices: 13.1 us -> none  [body(): gathered = lax.all_gather(packed, 'panel', axis=1, tiled=True)]
    all_to_all x0 -> x1, starting transfers between devices: none -> 4.86 us  [body(): lax.all_to_all(jnp.stack([packed] * lax.axis_size('panel')), 'panel', 0, 0)]
    reduce_scatter x1, waiting for transfers between devices: 105 us -> 101 us  [body(): lax.psum_scatter((product * scale).astype(jnp.bfloat16), 'tmc', scatter_d...]
    reshape x0 -> x1, local copies, waits for them, and re-layouts: none -> 4.51 us  [body(): jnp.concatenate(lax.all_to_all(jnp.stack([packed] * lax.axis_size('panel'...]
  transfers between devices with their start and end apart: 9 -> 9, of which waited for: 7 -> 7; matrix products, arithmetic and copies ran while one was open for 12% -> 11% of each run, Pallas kernels for 0% -> 0%
where the time goes in v1:
time: 279 us; the launch traced here: 278 us
  waiting for transfers between devices  136 us (49%)
  matrix products  36 us (13%)
  blocking collectives  30.8 us (11%)
  starting transfers between devices  24.8 us (9%)
  other arithmetic  20.3 us (7%)
  between operations  16.4 us (6%)
  local copies, waits for them, and re-layouts  14.2 us (5%)
    reduce_scatter x1, waiting for transfers between devices, body(): lax.psum_scatter((product * scale).astype(jnp.bfloat16), 'tmc', scatter_d...  101 us
    psum x1, blocking collectives, body(): lax.psum(right_part + lax.ppermute(right_part, 'core', swap), 'tmc')  30.8 us
    dot_general x1, matrix products, body(): lax.dot_general(row_side, col_side, (((0,), (0,)), ((), ())), preferred_e...  18.9 us
    all_to_all x1, waiting for transfers between devices, body(): lax.all_to_all(jnp.stack([packed] * lax.axis_size('panel')), 'panel', 0, 0)  16.8 us
    all_to_all x1, waiting for transfers between devices, body(): lax.all_to_all(send_design, TM, split_axis=0, concat_axis=0, tiled=True)  12.1 us
    all_to_all x1, starting transfers between devices, body(): lax.all_to_all(send_params, TM, split_axis=0, concat_axis=0, tiled=True)  9.43 us
    all_to_all x1, starting transfers between devices, body(): lax.all_to_all(send_design, TM, split_axis=0, concat_axis=0, tiled=True)  7.18 us
    another operation x3, other arithmetic, eliminate(): factor = jnp.linalg.cholesky(param_gram)  6.52 us
  transfers between devices with their start and end apart: 9, of which 7 were waited for; matrix products, arithmetic and copies ran while one was open for 11% of the time, Pallas kernels for 0%

profile of v1, /device:TPU:1, one launch (start us, length us, event | category | flops | bytes accessed | tf_op | source)
XLA Modules:
  0.0 278.3 jit_solution(612884135441769149)
XLA Ops:
  7.2 0.7 broadcast_in_dim.12
  7.9 0.5 broadcast.172
  8.5 2.3 fusion.53
  10.7 0.1 reshape_squeeze.3
  10.8 0.2 dynamic-slice_reduce_fusion
  11.0 0.2 convert_reduce_fusion
  11.2 1.0 convolution_convert_fusion.1
  12.2 0.1 copy.16
  12.3 0.8 reshape.162
  13.1 9.4 %all-to-all-start = ((bf16[32,2,390]{2,1,0:T(2,128)(2,1)}), bf16[32,2,390]{2,1,0:T(2,128)(2,1)S(1)}, u32[]{:S(2)}, u32[]{:S(2)}) async-start(bf16[32,2,390]{2,1,0:T(2,128)(2,1)} %reshape.162), calls=%async_computation | async-start | bytes 131072 | tf_op jit(solution)/shard_map/all_to_all | solution.py:73
  22.6 0.7 and_select_fusion
  23.3 0.1 iota_compare_fusion.11
  23.4 0.6 convolution_convert_fusion
  24.1 0.7 iota_compare_fusion.12
  24.7 0.6 dynamic_slice.13
  26.0 0.7 dynamic_slice.12
  28.1 0.1 add.105
  28.2 0.1 lt.73
  28.3 1.5 reshape.132
  29.7 0.2 all-to-all-done
  29.9 0.2 reshape.163
  30.1 7.2 %all-to-all-start.1 = ((bf16[32,12,1920]{2,1,0:T(8,128)(2,1)}), bf16[32,12,1920]{2,1,0:T(8,128)(2,1)S(1)}, u32[]{:S(2)}, u32[]{:S(2)}) async-start(bf16[32,12,1920]{2,1,0:T(8,128)(2,1)} %reshape.132), calls=%async_computation.1 | async-start | bytes 3932160 | tf_op jit(solution)/shard_map/all_to_all | solution.py:75
  37.4 0.7 fusion.34
  38.0 0.2 fusion.87
  38.3 0.2 slice_reduce_fusion
  38.5 0.1 copy.17
  38.6 5.8 %cholesky.17 = f32[64,64]{1,0:T(8,128)S(1)} custom-call(f32[64,64]{1,0:T(8,128)S(1)} %fusion.58), custom_call_target="Cholesky" | custom-call | tf_op jit(solution)/shard_map/jit(cholesky)/cholesky | solution.py:32
  44.5 0.6 compare_reduce_fusion
  45.1 0.7 fusion.52
  45.8 4.9 %custom-call.6 = f32[1,64,64]{1,2,0:T(8,128)S(1)} custom-call(f32[1,64,64]{2,1,0:T(8,128)S(1)} %fusion.52), custom_call_target="InvertDiagBlocksLowerTriangular" | custom-call | tf_op jit(solution)/shard_map/triangular_solve | solution.py:33
  50.7 0.3 fusion.84
  51.0 0.3 collective-permute-start.1
  51.3 0.6 convolution_bitcast_fusion
  52.0 0.2 convolution_bitcast_fusion.1
  52.1 12.1 %all-to-all-done.1 = bf16[32,12,1920]{2,1,0:T(8,128)(2,1)S(1)} async-done(((bf16[32,12,1920]{2,1,0:T(8,128)(2,1)}), bf16[32,12,1920]{2,1,0:T(8,128)(2,1)S(1)}, u32[]{:S(2)}, u32[]{:S(2)}) %all-to-all-start.1) | async-done | bytes 1474592 | tf_op jit(solution)/shard_map/all_to_all | solution.py:75
  64.2 1.3 reshape.134
  65.5 2.8 fusion.85
  68.3 0.1 slice.87
  68.4 1.8 fusion.88
  70.2 1.1 collective-permute-start
  71.3 0.4 convolution_reduce_fusion
  71.7 1.7 fusion.9
  73.4 0.1 fusion.27
  73.5 2.2 stack.2
  75.8 4.9 %all-to-all-start.2 = ((bf16[4,272,1920]{2,1,0:T(8,128)(2,1)}), bf16[4,272,1920]{2,1,0:T(8,128)(2,1)}, u32[]{:S(2)}, u32[]{:S(2)}) async-start(bf16[4,272,1920]{2,1,0:T(8,128)(2,1)} %stack.2), calls=%async_computation.2 | async-start | bytes 8355840 | tf_op jit(solution)/shard_map/all_to_all | solution.py:105
  80.7 0.1 collective-permute-start.2
  80.8 1.2 collective-permute-done.2
  82.0 30.8 %psum.7 = f32[1920]{0:T(1024)} all-reduce(f32[1920]{0:T(1024)S(1)} %add.114), channel_id=1, replica_groups=mesh['tmc'=16,'core'=2,'panel'=4] {'tmc'}, use_global_device_ids=true, to_apply=%region_6.7 | all-reduce | flops 1920 | bytes 15360 | tf_op jit(solution)/shard_map/psum | solution.py:107
  112.7 16.8 %all-to-all-done.2 = bf16[4,272,1920]{2,1,0:T(8,128)(2,1)} async-done(((bf16[4,272,1920]{2,1,0:T(8,128)(2,1)}), bf16[4,272,1920]{2,1,0:T(8,128)(2,1)}, u32[]{:S(2)}, u32[]{:S(2)}) %all-to-all-start.2) | async-done | bytes 4177952 | tf_op jit(solution)/shard_map/all_to_all | solution.py:105
  129.5 4.5 %copy.19 = bf16[4,34,8,1920]{3,2,0,1:T(8,128)(2,1)} copy(bf16[4,34,8,1920]{3,2,1,0:T(8,128)(2,1)} %bitcast.10) | data formatting | bytes 8355840 | tf_op jit(solution)/shard_map/reshape | solution.py:104
  134.0 0.8 collective-permute-start.3
  134.8 0.1 slice.93
  134.9 0.1 slice.94
  135.0 0.1 fusion.43
  135.1 3.4 %fusion.46 = f32[128,7680]{1,0:T(8,128)S(1)} fusion(bf16[272,7680]{1,0:T(8,128)(2,1)} %bitcast.11, bf16[128,544]{1,0:T(8,128)(2,1)S(1)} %fusion.43), kind=kOutput, calls=%fused_computation.70 | convolution fusion | flops 534773760 | bytes 8208384 | tf_op jit(solution)/shard_map/dot_general | solution.py:128
  138.4 3.5 %collective-permute-done.3 = bf16[272,7680]{1,0:T(8,128)(2,1)} collective-permute-done((bf16[272,7680]{1,0:T(8,128)(2,1)}, bf16[272,7680]{1,0:T(8,128)(2,1)}, u32[]{:S(2)}, u32[]{:S(2)}) %collective-permute-start.3) | collective-permute-done | bytes 4177952 | tf_op jit(solution)/shard_map/ppermute | solution.py:110
  141.9 3.4 %fusion.86 = (bf16[128,7680]{1,0:T(8,128)(2,1)S(1)}, bf16[128,7680]{1,0:T(8,128)(2,1)S(1)}) fusion(f32[128,7680]{1,0:T(8,128)S(1)} %fusion.46, bf16[272,7680]{1,0:T(8,128)(2,1)} %collective-permute-done.3, bf16[128,544]{1,0:T(8,128)(2,1)S(1)} %fusion.43), kind=kOutput, calls=%fused_computation.127 | convolution fusion | flops 537722880 | bytes 12140544 | tf_op jit(solution)/shard_map/dot_general | solution.py:129
  145.3 18.9 %multiply_convert_fusion = bf16[7680,960]{1,0:T(8,128)(2,1)} fusion(bf16[272,7680]{1,0:T(8,128)(2,1)} %collective-permute-done.3, bf16[272,7680]{1,0:T(8,128)(2,1)} %bitcast.11, bf16[128,7680]{1,0:T(8,128)(2,1)S(1)} %get-tuple-element.38, s32[]{:T(128)S(6)} %select_n.64, bf16[128,7680]{1,0:T(8,128)(2,1)S(1)} %get-tuple-element.39), kind=kOutput, calls=%fused_computation | convolution fusion | flops 9958625280 | bytes 35389444 | tf_op jit(solution)/shard_map/dot_general | solution.py:138
  164.3 100.7 %reduce-scatter.2.cloned.1.call-done = bf16[480,960]{1,0:T(8,128)(2,1)} async-done(((bf16[7680,960]{1,0:T(8,128)(2,1)}), bf16[480,960]{1,0:T(8,128)(2,1)}) %reduce-scatter.2.cloned.1.call-update) | async-done | bytes 921616 | tf_op jit(solution)/shard_map/reduce_scatter | solution.py:141
  265.0 1.2 broadcast_select_fusion.2
  266.2 1.0 collective-permute-start.4
  267.3 1.5 collective-permute-done.4
  268.7 1.3 broadcast_select_fusion.1
  270.0 1.5 maximum_convert_fusion
  (22 shorter events, 0.4 us)
Async XLA Ops:
  7.2 16.3 %copy-start = (bf16[256,1920]{1,0:T(8,128)(2,1)S(1)}, bf16[256,1920]{1,0:T(8,128)(2,1)}, u32[]{:S(2)}) copy-start(bf16[256,1920]{1,0:T(8,128)(2,1)} %param.8) | copy-start | bytes 2949124
  7.2 17.6 %copy-start.1 = (f32[32]{0:T(128)S(1)}, f32[32]{0:T(128)}, u32[]{:S(2)}) copy-start(f32[32]{0:T(128)} %param.13) | copy-start | bytes 388
  7.2 18.8 %copy-start.2 = (f32[32]{0:T(128)S(1)}, f32[32]{0:T(128)}, u32[]{:S(2)}) copy-start(f32[32]{0:T(128)} %param.12) | copy-start | bytes 388
  13.1 16.8 %all-to-all-start = ((bf16[32,2,390]{2,1,0:T(2,128)(2,1)}), bf16[32,2,390]{2,1,0:T(2,128)(2,1)S(1)}, u32[]{:S(2)}, u32[]{:S(2)}) async-start(bf16[32,2,390]{2,1,0:T(2,128)(2,1)} %reshape.162), calls=%async_computation | async-start | bytes 131072 | tf_op jit(solution)/shard_map/all_to_all | solution.py:73
  30.1 34.1 %all-to-all-start.1 = ((bf16[32,12,1920]{2,1,0:T(8,128)(2,1)}), bf16[32,12,1920]{2,1,0:T(8,128)(2,1)S(1)}, u32[]{:S(2)}, u32[]{:S(2)}) async-start(bf16[32,12,1920]{2,1,0:T(8,128)(2,1)} %reshape.132), calls=%async_computation.1 | async-start | bytes 3932160 | tf_op jit(solution)/shard_map/all_to_all | solution.py:75
  51.0 22.5 %collective-permute-start.1 = (bf16[64,384]{1,0:T(8,128)(2,1)S(1)}, bf16[64,384]{1,0:T(8,128)(2,1)S(1)}, u32[]{:S(2)}, u32[]{:S(2)}) collective-permute-start(bf16[64,384]{1,0:T(8,128)(2,1)S(1)} %get-tuple-element.33), channel_id=1, source_target_pairs={{0,4},{4,0},{1,5},{5,1},{2,6},{6,2},{3,7},{7,3},{8,12},{12,8},{9,1... | collective-permute-start | bytes 147464 | tf_op jit(solution)/shard_map/ppermute | solution.py:102
  70.2 3.2 %collective-permute-start = (bf16[112,1920]{1,0:T(8,128)(2,1)S(1)}, bf16[112,1920]{1,0:T(8,128)(2,1)S(1)}, u32[]{:S(2)}, u32[]{:S(2)}) collective-permute-start(bf16[112,1920]{1,0:T(8,128)(2,1)S(1)} %slice.89), channel_id=1, source_target_pairs={{0,4},{4,0},{1,5},{5,1},{2,6},{6,2},{3,7},{7,3},{8,12},{12,8},{9,1... | collective-permute-start | bytes 1290248 | tf_op jit(solution)/shard_map/ppermute | solution.py:100
  75.8 53.7 %all-to-all-start.2 = ((bf16[4,272,1920]{2,1,0:T(8,128)(2,1)}), bf16[4,272,1920]{2,1,0:T(8,128)(2,1)}, u32[]{:S(2)}, u32[]{:S(2)}) async-start(bf16[4,272,1920]{2,1,0:T(8,128)(2,1)} %stack.2), calls=%async_computation.2 | async-start | bytes 8355840 | tf_op jit(solution)/shard_map/all_to_all | solution.py:105
  80.7 184.3 %reduce-scatter.2.cloned.1.call-start = ((), (), s32[]{:S(2)}) async-start(), calls=%async_computation.4 | async-start | bytes 16711680 | tf_op jit(solution)/shard_map/reduce_scatter | solution.py:141
  80.7 1.3 collective-permute-start.2
  134.0 7.9 %collective-permute-start.3 = (bf16[272,7680]{1,0:T(8,128)(2,1)}, bf16[272,7680]{1,0:T(8,128)(2,1)}, u32[]{:S(2)}, u32[]{:S(2)}) collective-permute-start(bf16[272,7680]{1,0:T(8,128)(2,1)} %bitcast.11), channel_id=1, source_target_pairs={{0,4},{4,0},{1,5},{5,1},{2,6},{6,2},{3,7},{7,3},{8,12},{12,8},{9,1... | collective-permute-start | bytes 12533768 | tf_op jit(solution)/shard_map/ppermute | solution.py:110
  266.2 2.5 collective-permute-start.4
Sparse Core Ops, SparseCore 0:
  164.4 100.5 reduce-scatter.1
